TPU v7x, 32 devices: a whole 2x2x4 slice. The times are simulated.
32 devices in a mesh: lat: 4 (over x, core), lon: 8 (over z, y).
Axes of the slice: x: 2, y: 2, z: 4, core: 2. Of those that a mesh axis runs over, the one named last changes fastest.
Arguments:
- nodes: bfloat16 [4, 8, 384, 512], P('lat', 'lon'), may hold values from -6 to 6
- edges: bfloat16 [4, 8, 3072, 512], P('lat', 'lon'), may hold values from -6 to 6
- senders: int32 [4, 8, 3072], P('lat', 'lon'), may hold values from 0 to 511, as said below
- receivers: int32 [4, 8, 3072], P('lat', 'lon'), may hold values from 0 to 383
- edge_count: int32 [4, 8], P('lat', 'lon'), may hold values from 1536 to 3072, as said below
- halo_send: int32 [4, 8, 4, 24], P('lat', 'lon'), may hold values from 0 to 383
- long_need: int32 [4, 8, 32, 1], P('lat', 'lon'), may hold values from 0 to 1
- node_cot: bfloat16 [4, 8, 384, 512], P('lat', 'lon'), may hold values from -6 to 6
- edge_cot: bfloat16 [4, 8, 3072, 512], P('lat', 'lon'), may hold values from -6 to 6
- e_w1: bfloat16 [1536, 512], replicated, may hold values from -0.15625 to 0.15625
- e_b1: float32 [512], replicated, may hold values from -3 to 3
- e_w2: bfloat16 [512, 512], replicated, may hold values from -0.25 to 0.25
- e_gain: float32 [512], replicated, may hold values from 0.25 to 1.75
- n_w1: bfloat16 [1024, 512], replicated, may hold values from -0.1875 to 0.1875
- n_b1: float32 [512], replicated, may hold values from -3 to 3
- n_w2: bfloat16 [512, 512], replicated, may hold values from -0.25 to 0.25
- n_gain: float32 [512], replicated, may hold values from 0.25 to 1.75
Outputs:
- new_nodes: bfloat16 [4, 8, 384, 512], P('lat', 'lon')
- new_edges: bfloat16 [4, 8, 3072, 512], P('lat', 'lon')
- node_grad: float32 [4, 8, 384, 512], P('lat', 'lon')
- edge_grad: float32 [4, 8, 3072, 512], P('lat', 'lon')
- e_w1_grad: float32 [1536, 512], P(('lat', 'lon'))
- e_b1_grad: float32 [512], P(('lat', 'lon'))
- e_w2_grad: float32 [512, 512], P(('lat', 'lon'))
- e_gain_grad: float32 [512], P(('lat', 'lon'))
- n_w1_grad: float32 [1024, 512], P(('lat', 'lon'))
- n_b1_grad: float32 [512], P(('lat', 'lon'))
- n_w2_grad: float32 [512, 512], P(('lat', 'lon'))
- n_gain_grad: float32 [512], P(('lat', 'lon'))
Inputs may be any that keep to these rules, and one draw needn't show every extreme that they name: `senders`: entries below 384 are a region's own nodes, the next 96 the four neighbour blocks, the rest the coarse rows; the third block is never named in the first band and the fourth never in the last. The first three edge slots of region r name the coarse rows of regions r + 1, r - 1 and r + 16 in flat order, counted round. `edge_count`: some region has all 3072 slots live. `long_need`: A region's coarse nodes are its first 2 rows.
All inputs are finite; a program needn't handle non-finite values.
Results may differ from a plain program's by a relative error of at most 0.009.
Values may be sent and summed in bfloat16 or wider, within the bound.
A program may use at most 192 MiB of HBM per device.

v0:
```python
import jax
import jax.numpy as jnp
from jax import lax
from jax.sharding import PartitionSpec as P

COARSE = 2


EPS = 1e-05


def shifted(block, axis, distance):
    devices = range(lax.axis_size(axis))
    route = [((i - distance) % len(devices), i) for i in devices]
    return lax.ppermute(block, axis, route)


def passed_along(value, axis, steps):
    count = lax.axis_size(axis)
    leading, last = (max(0, -steps), min(count, count - steps))
    return lax.ppermute(value, axis, [(source, source + steps) for source in range(leading, last)])


def layer_norm(z, gain):
    mean = jnp.mean(z, axis=-1, keepdims=True)
    centred = z - mean
    rstd = lax.rsqrt(jnp.mean(centred * centred, axis=-1, keepdims=True) + EPS)
    normed = centred * rstd
    return (normed * gain, normed, rstd)


def transposed(left, right):
    return lax.dot_general(
        left, right, (((0,), (0,)), ((), ())), preferred_element_type=jnp.float32
    )


def mlp_forward(parts, w_first, b_first, w_second, gain):
    width = parts[0].shape[1]
    z_first = b_first
    for number, piece in enumerate(parts):
        z_first = z_first + jnp.dot(
            piece,
            w_first[number * width : (number + 1) * width],
            preferred_element_type=jnp.float32,
        )
    active = jax.nn.silu(z_first).astype(jnp.bfloat16)
    z_second = jnp.dot(active, w_second, preferred_element_type=jnp.float32)
    result, normed, rstd = layer_norm(z_second, gain)
    return (result, (z_first, active, normed, rstd))


def mlp_backward(parts, saved, grad_out, w_first, w_second, gain):
    z_first, active, normed, rstd = saved
    gain_grad = jnp.sum(grad_out * normed, axis=0)
    scaled = grad_out * gain
    g_second = rstd * (
        scaled
        - jnp.mean(scaled, axis=-1, keepdims=True)
        - normed * jnp.mean(scaled * normed, axis=-1, keepdims=True)
    )
    g_second = g_second.astype(jnp.bfloat16)
    second_grad = transposed(active, g_second)
    g_active = jnp.dot(g_second, w_second.T, preferred_element_type=jnp.float32)
    sigma = jax.nn.sigmoid(z_first)
    g_first = (g_active * sigma * (1.0 + z_first * (1.0 - sigma))).astype(jnp.bfloat16)
    bias_grad = jnp.sum(g_first, axis=0, dtype=jnp.float32)
    first_grad = jnp.concatenate([transposed(piece, g_first) for piece in parts], axis=0)
    g_input = jnp.dot(g_first, w_first.T, preferred_element_type=jnp.float32)
    return (g_input, (first_grad, bias_grad, second_grad, gain_grad))


def shards(
    nodes,
    edges,
    senders,
    receivers,
    edge_count,
    halo_send,
    long_need,
    node_cot,
    edge_cot,
    e_w1,
    e_b1,
    e_w2,
    e_gain,
    n_w1,
    n_b1,
    n_w2,
    n_gain,
):
    nodes_l = nodes[0, 0]
    edges_l = edges[0, 0]
    snd = senders[0, 0]
    rcv = receivers[0, 0]
    count = edge_count[0, 0]
    rows_out = halo_send[0, 0]
    need = long_need[0, 0]
    node_n, width = nodes_l.shape
    halo_n = rows_out.shape[1]
    devices, slot_n = need.shape
    sent = jnp.take(nodes_l, rows_out, axis=0)
    from_east = shifted(sent[0], "lon", 1)
    from_west = shifted(sent[1], "lon", -1)
    from_north = passed_along(sent[2], "lat", 1)
    from_south = passed_along(sent[3], "lat", -1)
    wanted = lax.all_to_all(need, ("lat", "lon"), split_axis=0, concat_axis=0, tiled=True)
    outgoing = jnp.take(nodes_l, wanted, axis=0)
    far = lax.all_to_all(outgoing, ("lat", "lon"), split_axis=0, concat_axis=0, tiled=True).reshape(
        devices * slot_n, width
    )
    table = jnp.concatenate([nodes_l, from_east, from_west, from_north, from_south, far], axis=0)
    recv_rows = jnp.take(nodes_l, rcv, axis=0)
    sent_rows = jnp.take(table, snd, axis=0)
    edge_parts = (edges_l, sent_rows, recv_rows)
    edge_out, edge_saved = mlp_forward(edge_parts, e_w1, e_b1, e_w2, e_gain)
    alive = jnp.arange(edges_l.shape[0]) < count
    live = alive.astype(jnp.float32)[:, None]
    new_edges = (edges_l + live * edge_out).astype(jnp.bfloat16)
    recv_table = ((rcv[None, :] == jnp.arange(node_n)[:, None]) & alive[None, :]).astype(
        jnp.bfloat16
    )
    aggregate = jnp.dot(recv_table, new_edges, preferred_element_type=jnp.float32).astype(
        jnp.bfloat16
    )
    node_parts = (nodes_l, aggregate)
    node_out, node_saved = mlp_forward(node_parts, n_w1, n_b1, n_w2, n_gain)
    new_nodes = (nodes_l + node_out).astype(jnp.bfloat16)
    node_up = node_cot[0, 0].astype(jnp.float32)
    g_node_in, node_grads = mlp_backward(node_parts, node_saved, node_up, n_w1, n_w2, n_gain)
    n_first, n_bias, n_second, n_scale = node_grads
    node_sums = (
        lax.psum_scatter(n_first, ("lat", "lon"), scatter_dimension=0, tiled=True),
        lax.psum_scatter(n_bias, ("lat", "lon"), scatter_dimension=0, tiled=True),
        lax.psum_scatter(n_second, ("lat", "lon"), scatter_dimension=0, tiled=True),
        lax.psum_scatter(n_scale, ("lat", "lon"), scatter_dimension=0, tiled=True),
    )
    g_aggregate = g_node_in[:, width:]
    g_new_edges = edge_cot[0, 0].astype(jnp.float32) + live * jnp.take(g_aggregate, rcv, axis=0)
    g_edge_in, edge_grads = mlp_backward(
        edge_parts, edge_saved, live * g_new_edges, e_w1, e_w2, e_gain
    )
    e_first, e_bias, e_second, e_scale = edge_grads
    g_edge_in = g_edge_in.astype(jnp.bfloat16)
    edge_grad = g_new_edges + g_edge_in[:, :width]
    send_table = (snd[None, :] == jnp.arange(table.shape[0])[:, None]).astype(jnp.bfloat16)
    sender_grad = jnp.dot(
        send_table, g_edge_in[:, width : 2 * width], preferred_element_type=jnp.float32
    )
    halo_part = sender_grad[node_n : node_n + 4 * halo_n]
    to_east = shifted(halo_part[:halo_n].astype(jnp.bfloat16), "lon", -1).astype(jnp.float32)
    to_west = shifted(halo_part[halo_n : 2 * halo_n].astype(jnp.bfloat16), "lon", 1).astype(
        jnp.float32
    )
    to_north = passed_along(
        halo_part[2 * halo_n : 3 * halo_n].astype(jnp.bfloat16), "lat", -1
    ).astype(jnp.float32)
    to_south = passed_along(halo_part[3 * halo_n :].astype(jnp.bfloat16), "lat", 1).astype(
        jnp.float32
    )
    far_grad = sender_grad[node_n + 4 * halo_n :]
    came = (
        lax.all_to_all(
            far_grad.reshape(devices, slot_n, width).astype(jnp.bfloat16),
            ("lat", "lon"),
            split_axis=0,
            concat_axis=0,
            tiled=True,
        )
        .astype(jnp.float32)
        .reshape(devices * slot_n, width)
    )
    coarse_table = (wanted.reshape(-1)[None, :] == jnp.arange(COARSE)[:, None]).astype(jnp.float32)
    coarse_grad = jnp.dot(
        coarse_table, came, precision=lax.Precision.HIGHEST, preferred_element_type=jnp.float32
    )
    returned = jnp.concatenate([to_east, to_west, to_north, to_south], axis=0)
    border_table = (rows_out.reshape(-1)[None, :] == jnp.arange(node_n)[:, None]).astype(
        jnp.float32
    )
    node_grad = (
        node_up
        + g_node_in[:, :width]
        + jnp.dot(recv_table, g_edge_in[:, 2 * width :], preferred_element_type=jnp.float32)
    )
    node_grad = node_grad + sender_grad[:node_n]
    node_grad = node_grad + jnp.dot(
        border_table, returned, precision=lax.Precision.HIGHEST, preferred_element_type=jnp.float32
    )
    node_grad = node_grad + jnp.pad(coarse_grad, ((0, node_n - COARSE), (0, 0)))
    edge_sums = (
        lax.psum_scatter(e_first, ("lat", "lon"), scatter_dimension=0, tiled=True),
        lax.psum_scatter(e_bias, ("lat", "lon"), scatter_dimension=0, tiled=True),
        lax.psum_scatter(e_second, ("lat", "lon"), scatter_dimension=0, tiled=True),
        lax.psum_scatter(e_scale, ("lat", "lon"), scatter_dimension=0, tiled=True),
    )
    sums = edge_sums + node_sums
    return (
        new_nodes[None, None],
        new_edges[None, None],
        node_grad[None, None],
        edge_grad[None, None],
        sums[0],
        sums[1],
        sums[2],
        sums[3],
        sums[4],
        sums[5],
        sums[6],
        sums[7],
    )


def solution(mesh):
    return jax.shard_map(
        shards,
        mesh=mesh,
        in_specs=(
            P("lat", "lon", None, None),
            P("lat", "lon", None, None),
            P("lat", "lon", None),
            P("lat", "lon", None),
            P("lat", "lon"),
            P("lat", "lon", None, None),
            P("lat", "lon", None, None),
            P("lat", "lon", None, None),
            P("lat", "lon", None, None),
            P(),
            P(),
            P(),
            P(),
            P(),
            P(),
            P(),
            P(),
        ),
        out_specs=(
            P("lat", "lon", None, None),
            P("lat", "lon", None, None),
            P("lat", "lon", None, None),
            P("lat", "lon", None, None),
            P(("lat", "lon"), None),
            P(("lat", "lon")),
            P(("lat", "lon"), None),
            P(("lat", "lon")),
            P(("lat", "lon"), None),
            P(("lat", "lon")),
            P(("lat", "lon"), None),
            P(("lat", "lon")),
        ),
        check_vma=False,
    )
```

profile of v0, /device:TPU:0, one launch (start us, length us, event | category | flops | bytes accessed | tf_op | source)
XLA Modules:
  0.0 695.9 jit_solution(10908704420119605315)
XLA Ops:
  7.2 1.4 copy.57
  8.6 7.3 %all-to-all-start = ((s32[32,1,1]{2,1,0:T(1,128)}), s32[32,1,1]{2,1,0:T(1,128)S(1)}, u32[]{:S(2)}, u32[]{:S(2)}) async-start(s32[32,1,1]{2,1,0:T(1,128)} %copy.57), calls=%async_computation | async-start | bytes 32768 | tf_op jit(solution)/shard_map/all_to_all | solution.py:107
  17.4 1.0 constant_dynamic-update-slice_fusion.4
  21.3 4.7 copy.56
  26.0 6.6 fusion.11
  33.0 13.3 %gather_fusion.3 = bf16[3072,512]{1,0:T(8,128)(2,1)} fusion(bf16[384,512]{1,0:T(8,128)(2,1)S(1)} %bitcast.99, s32[3072]{0:T(1024)S(1)} %broadcast_clamp_fusion), kind=kCustom, calls=%fused_computation.3 | custom fusion | bytes 6303744 | tf_op jit(solution)/shard_map/jit(_take)/gather | solution.py:113
  46.3 4.7 copy.60
  51.0 4.6 copy.61
  55.6 1.2 and_reduce_fusion
  57.5 0.8 gather_fusion
  58.3 1.8 collective-permute-start
  60.2 3.0 collective-permute-start.1
  63.1 2.2 collective-permute-start.2
  65.4 1.3 collective-permute-start.3
  69.8 5.2 all-to-all-start.1
  75.1 0.7 constant_dynamic-update-slice_fusion.3
  75.8 0.7 constant_dynamic-update-slice_fusion.2
  78.0 4.2 all-to-all-done.1
  82.2 13.3 %gather_fusion.2 = bf16[3072,512]{1,0:T(8,128)(2,1)} fusion(bf16[512,512]{1,0:T(8,128)(2,1)S(1)} %bitcast_dynamic-update-slice_fusion, s32[3072]{0:T(1024)S(1)} %broadcast_clamp_fusion.1), kind=kCustom, calls=%fused_computation.2 | custom fusion | bytes 6303744 | tf_op jit(solution)/shard_map/jit(_take)/gather | solution.py:114
  95.5 4.8 copy.59
  100.3 4.0 fusion.15
  104.3 17.8 %multiply_convert_fusion.2 = (bf16[3072,512]{1,0:T(8,128)(2,1)S(1)}, f32[3072,512]{1,0:T(8,128)}) fusion(bf16[1536,512]{1,0:T(8,128)(2,1)} %param.26, bf16[3072,512]{0,1:T(8,128)(2,1)S(1)} %copy-done.12, pred[3072]{0:T(1024)(128)(4,1)S(1)} %get-tuple-element.97, f32[3072,512]{1,0:T(8,128)S(1)} %fusion.15, f32[3072,512]{1,0:T(8,128)} %fusion.11, ...), kind=kOutput, calls=%fused_computation.16 | convolution fusion | flops 1624768512 | bytes 25695232 | tf_op jit(solution)/shard_map/dot_general | solution.py:42
  122.1 1.9 fusion.84
  124.1 0.8 multiply_reduce_fusion.2
  124.9 2.4 copy-done.2
  127.2 1.0 copy-done.6
  128.2 1.8 add_convert_fusion
  130.0 1.4 fusion.42
  133.8 1.1 fusion.50
  136.3 1.2 copy-done.10
  137.5 12.9 %gather_fusion.4 = f32[3072,512]{1,0:T(8,128)} fusion(f32[384,512]{1,0:T(8,128)S(1)} %slice.105, s32[3072]{0:T(1024)S(1)} %broadcast_clamp_fusion), kind=kCustom, calls=%fused_computation.4 | custom fusion | bytes 12595200 | tf_op jit(solution)/shard_map/jit(_take)/gather | solution.py:139
  150.4 6.6 copy.62
  157.0 7.7 %multiply_reduce_fusion = (f32[512]{0:T(512)S(1)}, f32[3072]{0:T(1024)S(1)}, f32[3072]{0:T(1024)S(1)}, f32[3072,512]{0,1:T(8,128)S(1)}) fusion(f32[3072,512]{0,1:T(8,128)} %copy-done.2, f32[3072]{0:T(1024)S(1)} %add_rsqrt_fusion, f32[3072]{0:T(1024)S(1)} %broadcast_multiply_fusion.2, f32[3072]{0:T(1024)S(1)} %get-tuple-element.98, f32[512]{0:T(512)S(1)} %copy-done.28, ...), kind=kLoop, calls=%fused_computation.7 | loop fusion | flops 20440576 | bytes 22088704 | tf_op jit(solution)/shard_map/reduce_sum | solution.py:55
  164.7 6.2 multiply_convert_fusion.1
  170.9 1.7 copy-done.11
  172.6 2.9 fusion.88
  175.5 1.5 fusion.81
  178.1 1.6 pad_maximum_fusion.1
  180.5 7.1 %convert_reduce_fusion = (f32[512]{0:T(512)S(1)}, bf16[3072,512]{1,0:T(8,128)(2,1)S(1)}) fusion(f32[3072,512]{1,0:T(8,128)} %get-tuple-element.84, bf16[3072,512]{0,1:T(8,128)(2,1)} %copy-done.11, bf16[512,512]{1,0:T(8,128)(2,1)S(1)} %copy-done), kind=kOutput, calls=%fused_computation.8 | convolution fusion | flops 1627913728 | bytes 13109248 | tf_op jit(solution)/shard_map/dot_general | solution.py:64
  187.6 1.8 fusion.25
  189.4 1.2 copy-done.14
  190.6 1.8 fusion.14
  192.5 1.8 fusion.16
  194.3 2.0 pad_maximum_fusion
  196.3 1.4 copy-done.24
  197.7 7.2 %convolution_convert_fusion = bf16[3072,1536]{0,1:T(8,128)(2,1)S(1)} fusion(bf16[3072,512]{1,0:T(8,128)(2,1)} %copy-done.34, bf16[1536,512]{1,0:T(8,128)(2,1)S(1)} %copy-done.24), kind=kOutput, calls=%fused_computation.5 | convolution fusion | flops 4836556800 | bytes 14155776 | tf_op jit(solution)/shard_map/dot_general | solution.py:69
  205.0 2.8 fusion.86
  207.7 1.4 copy-done.18
  209.1 0.8 copy-done.27
  211.2 2.5 all-to-all-start.2
  213.7 4.8 fusion.36
  218.5 5.4 add_bitcast_fusion
  223.9 0.8 fusion.83
  224.7 40.7 %all-reduce.5 = (f32[512]{0:T(512)S(1)}, f32[512]{0:T(512)S(1)}, f32[512]{0:T(512)S(1)}, f32[512]{0:T(512)S(1)}) all-reduce(f32[512]{0:T(512)S(1)} %get-tuple-element.91, f32[512]{0:T(512)S(1)} %get-tuple-element.60, f32[512]{0:T(512)S(1)} %get-tuple-element.93, ...), channel_id=3, replica_groups=mesh['lat'=4,'lon'=8] {'lat','lon'}, use_global_device_ids=true, to_apply=%region_10.11.clone | all-reduce | flops 2048 | bytes 16384
  267.8 6.6 copy.66
  274.4 4.0 collective-permute-start.4
  278.4 1.3 collective-permute-start.6
  279.7 3.0 collective-permute-start.7
  282.7 4.7 copy.65
  287.6 1.1 fusion.30
  288.8 21.0 %reduce-scatter.7.cloned.1.call-done = f32[16,512]{1,0:T(8,128)} async-done(((f32[512,512]{1,0:T(8,128)}), f32[16,512]{1,0:T(8,128)}) %reduce-scatter.7.cloned.1.call-update) | async-done | bytes 32784 | tf_op jit(solution)/shard_map/reduce_scatter | solution.py:194
  309.7 136.0 %reduce-scatter.11.cloned.1.call-done = f32[16,512]{1,0:T(8,128)} async-done(((f32[512,512]{1,0:T(8,128)}), f32[16,512]{1,0:T(8,128)}) %reduce-scatter.11.cloned.1.call-update) | async-done | bytes 32784 | tf_op jit(solution)/shard_map/reduce_scatter | solution.py:135
  445.8 138.5 %reduce-scatter.9.cloned.1.call-done = f32[32,512]{1,0:T(8,128)} async-done(((f32[1024,512]{1,0:T(8,128)}), f32[32,512]{1,0:T(8,128)}) %reduce-scatter.9.cloned.1.call-update) | async-done | bytes 65552 | tf_op jit(solution)/shard_map/reduce_scatter | solution.py:133
  584.2 104.7 %reduce-scatter.5.cloned.1.call-done = f32[48,512]{1,0:T(8,128)} async-done(((f32[1536,512]{1,0:T(8,128)}), f32[48,512]{1,0:T(8,128)}) %reduce-scatter.5.cloned.1.call-update) | async-done | bytes 98320 | tf_op jit(solution)/shard_map/reduce_scatter | solution.py:192
  (138 shorter events, 19.0 us)
Async XLA Ops:
  7.2 114.9 %copy-start = (bf16[512,512]{1,0:T(8,128)(2,1)S(1)}, bf16[512,512]{1,0:T(8,128)(2,1)}, u32[]{:S(2)}) copy-start(bf16[512,512]{1,0:T(8,128)(2,1)} %param.28) | copy-start | bytes 1572868
  8.6 47.0 %all-to-all-start = ((s32[32,1,1]{2,1,0:T(1,128)}), s32[32,1,1]{2,1,0:T(1,128)S(1)}, u32[]{:S(2)}, u32[]{:S(2)}) async-start(s32[32,1,1]{2,1,0:T(1,128)} %copy.57), calls=%async_computation | async-start | bytes 32768 | tf_op jit(solution)/shard_map/all_to_all | solution.py:107
  26.0 6.6 copy-start.25
  26.0 6.6 copy-start.1
  26.0 6.7 copy-start.9
  26.0 6.7 copy-start.31
  58.3 16.7 %collective-permute-start = (bf16[24,512]{1,0:T(8,128)(2,1)S(1)}, bf16[24,512]{1,0:T(8,128)(2,1)}, u32[]{:S(2)}, u32[]{:S(2)}) collective-permute-start(bf16[24,512]{1,0:T(8,128)(2,1)S(1)} %get-tuple-element.82), channel_id=1, source_target_pairs={{7,0},{0,1},{1,2},{2,3},{3,4},{4,5},{5,6},{6,7},{15,8},{8,9},{9,10... | collective-permute-start | bytes 73736 | tf_op jit(solution)/shard_map/ppermute | solution.py:15
  60.2 15.6 %collective-permute-start.1 = (bf16[24,512]{1,0:T(8,128)(2,1)S(1)}, bf16[24,512]{1,0:T(8,128)(2,1)}, u32[]{:S(2)}, u32[]{:S(2)}) collective-permute-start(bf16[24,512]{1,0:T(8,128)(2,1)S(1)} %get-tuple-element.81), channel_id=1, source_target_pairs={{1,0},{2,1},{3,2},{4,3},{5,4},{6,5},{7,6},{0,7},{9,8},{10,9},{11,1... | collective-permute-start | bytes 73736 | tf_op jit(solution)/shard_map/ppermute | solution.py:15
  63.1 13.4 %collective-permute-start.2 = (bf16[24,512]{1,0:T(8,128)(2,1)S(1)}, bf16[24,512]{1,0:T(8,128)(2,1)}, u32[]{:S(2)}, u32[]{:S(2)}) collective-permute-start(bf16[24,512]{1,0:T(8,128)(2,1)S(1)} %get-tuple-element.80), channel_id=1, source_target_pairs={{0,8},{8,16},{16,24},{1,9},{9,17},{17,25},{2,10},{10,18},{18,26},{... | collective-permute-start | bytes 73736 | tf_op jit(solution)/shard_map/ppermute | solution.py:21
  65.4 11.9 %collective-permute-start.3 = (bf16[24,512]{1,0:T(8,128)(2,1)S(1)}, bf16[24,512]{1,0:T(8,128)(2,1)}, u32[]{:S(2)}, u32[]{:S(2)}) collective-permute-start(bf16[24,512]{1,0:T(8,128)(2,1)S(1)} %get-tuple-element.79), channel_id=1, source_target_pairs={{8,0},{16,8},{24,16},{9,1},{17,9},{25,17},{10,2},{18,10},{26,18},{... | collective-permute-start | bytes 73736 | tf_op jit(solution)/shard_map/ppermute | solution.py:21
  69.8 12.4 %all-to-all-start.1 = ((bf16[32,2,256]{2,1,0:T(2,128)(2,1)}), bf16[32,2,256]{2,1,0:T(2,128)(2,1)S(1)}, u32[]{:S(2)}, u32[]{:S(2)}) async-start(bf16[32,2,256]{2,1,0:T(2,128)(2,1)} %reshape.306), calls=%async_computation.1 | async-start | bytes 65536 | tf_op jit(solution)/shard_map/all_to_all | solution.py:109
  75.0 234.7 %reduce-scatter.7.cloned.1.call-start = ((), (), s32[]{:S(2)}) async-start(), calls=%async_computation.8 | async-start | bytes 1081344 | tf_op jit(solution)/shard_map/reduce_scatter | solution.py:194
  100.3 4.0 copy-start.12
  100.3 4.0 copy-start.33
  122.1 2.0 copy-start.7
  124.0 3.2 copy-start.2
  124.1 4.2 copy-start.6
  124.1 4.2 copy-start.28
  130.0 1.7 copy-start.5
  130.0 2.0 copy-start.32
  131.6 0.9 copy-start.15
  132.0 2.9 copy-start.19
  132.0 1.3 copy-start.17
  132.0 1.3 copy-start.30
  134.9 0.8 copy-start.22
  136.2 1.2 copy-start.10
  164.7 6.2 copy-start.3
  164.7 7.8 %copy-start.8 = (bf16[3072,512]{1,0:T(8,128)(2,1)S(1)}, bf16[3072,512]{1,0:T(8,128)(2,1)}, u32[]{:S(2)}) copy-start(bf16[3072,512]{1,0:T(8,128)(2,1)} %copy-done.7) | copy-start | bytes 9437188
  170.9 1.7 copy-start.11
  172.6 2.9 copy-start.20
  172.6 2.9 copy-start.23
  175.4 1.7 copy-start.16
  175.5 270.3 %reduce-scatter.11.cloned.1.call-start = ((), (), s32[]{:S(2)}) async-start(), calls=%async_computation.10 | async-start | bytes 1081344 | tf_op jit(solution)/shard_map/reduce_scatter | solution.py:135
  177.0 407.2 %reduce-scatter.9.cloned.1.call-start = ((), (), s32[]{:S(2)}) async-start(), calls=%async_computation.9 | async-start | bytes 2162688 | tf_op jit(solution)/shard_map/reduce_scatter | solution.py:133
  178.0 1.7 copy-start.29
  179.7 509.2 %reduce-scatter.5.cloned.1.call-start = ((), (), s32[]{:S(2)}) async-start(), calls=%async_computation.7 | async-start | bytes 3244032 | tf_op jit(solution)/shard_map/reduce_scatter | solution.py:192
  180.5 7.1 %copy-start.4 = (bf16[1,1,3072,512]{3,2,1,0:T(8,128)(2,1)S(1)}, bf16[1,1,3072,512]{3,2,1,0:T(8,128)(2,1)}, u32[]{:S(2)}) copy-start(bf16[1,1,3072,512]{3,2,1,0:T(8,128)(2,1)} %param.18) | copy-start | bytes 9437188
  187.6 4.9 copy-start.34
  187.6 3.0 copy-start.14
  190.6 1.9 copy-start.13
  196.3 1.4 copy-start.24
  197.7 7.2 %copy-start.26 = (s32[1,1,3072]{2,1,0:T(1,128)S(1)}, s32[1,1,3072]{2,1,0:T(1,128)}, u32[]{:S(2)}) copy-start(s32[1,1,3072]{2,1,0:T(1,128)} %param.19) | copy-start | bytes 36868
  204.9 4.2 copy-start.18
  204.9 13.6 %slice-start = ((s8[6291456]{0:T(1024)(128)(4,1)}), s8[2097152]{0:T(1024)(128)(4,1)S(1)}, s32[]{:S(2)}) async-start(s8[6291456]{0:T(1024)(128)(4,1)} %bitcast.102), calls=%async_computation.11 | async-start | bytes 4194304
  209.1 0.8 copy-start.27
  211.2 76.2 %all-to-all-start.2 = ((bf16[32,2,256]{2,1,0:T(2,128)(2,1)}), bf16[32,2,256]{2,1,0:T(2,128)(2,1)S(1)}, u32[]{:S(2)}, u32[]{:S(2)}) async-start(bf16[32,2,256]{2,1,0:T(2,128)(2,1)} %reshape.308), calls=%async_computation.2 | async-start | bytes 65536 | tf_op jit(solution)/shard_map/all_to_all | solution.py:163
  213.7 4.8 slice-start.1
  274.4 13.2 %collective-permute-start.4 = (bf16[24,512]{1,0:T(8,128)(2,1)S(1)}, bf16[24,512]{1,0:T(8,128)(2,1)S(1)}, u32[]{:S(2)}, u32[]{:S(2)}) collective-permute-start(bf16[24,512]{1,0:T(8,128)(2,1)S(1)} %get-tuple-element.75), channel_id=1, source_target_pairs={{1,0},{2,1},{3,2},{4,3},{5,4},{6,5},{7,6},{0,7},{9,8},{10,9},{11,1... | collective-permute-start | bytes 73736 | tf_op jit(solution)/shard_map/ppermute | solution.py:15
  278.4 9.2 %collective-permute-start.5 = (bf16[24,512]{1,0:T(8,128)(2,1)S(1)}, bf16[24,512]{1,0:T(8,128)(2,1)S(1)}, u32[]{:S(2)}, u32[]{:S(2)}) collective-permute-start(bf16[24,512]{1,0:T(8,128)(2,1)S(1)} %get-tuple-element.78), channel_id=1, source_target_pairs={{7,0},{0,1},{1,2},{2,3},{3,4},{4,5},{5,6},{6,7},{15,8},{8,9},{9,10... | collective-permute-start | bytes 73736 | tf_op jit(solution)/shard_map/ppermute | solution.py:15
  278.4 9.2 %collective-permute-start.6 = (bf16[24,512]{1,0:T(8,128)(2,1)S(1)}, bf16[24,512]{1,0:T(8,128)(2,1)S(1)}, u32[]{:S(2)}, u32[]{:S(2)}) collective-permute-start(bf16[24,512]{1,0:T(8,128)(2,1)S(1)} %get-tuple-element.77), channel_id=1, source_target_pairs={{8,0},{16,8},{24,16},{9,1},{17,9},{25,17},{10,2},{18,10},{26,18},{... | collective-permute-start | bytes 73736 | tf_op jit(solution)/shard_map/ppermute | solution.py:21
  279.7 7.9 %collective-permute-start.7 = (bf16[24,512]{1,0:T(8,128)(2,1)S(1)}, bf16[24,512]{1,0:T(8,128)(2,1)S(1)}, u32[]{:S(2)}, u32[]{:S(2)}) collective-permute-start(bf16[24,512]{1,0:T(8,128)(2,1)S(1)} %get-tuple-element.76), channel_id=1, source_target_pairs={{0,8},{8,16},{16,24},{1,9},{9,17},{17,25},{2,10},{10,18},{18,26},{... | collective-permute-start | bytes 73736 | tf_op jit(solution)/shard_map/ppermute | solution.py:21
  282.7 4.9 copy-start.21
Sparse Core Ops, SparseCore 0:
  175.6 134.1 reduce-scatter.6
  312.6 133.1 reduce-scatter.10
  448.6 135.5 reduce-scatter.8
  590.1 98.8 reduce-scatter.4
where the time goes:
time: 699 us; the launch traced here: 696 us
  waiting for transfers between devices  404 us (58%)
  local copies, waits for them, and re-layouts  100 us (14%)
  matrix products  67.9 us (10%)
  blocking collectives  40.7 us (6%)
  other arithmetic  35.4 us (5%)
  starting transfers between devices  31.8 us (5%)
  between operations  15.5 us (2%)
    reduce_scatter x1, waiting for transfers between devices, shards(): lax.psum_scatter(n_first, ('lat', 'lon'), scatter_dimension=0, tiled=True)  138 us
    reduce_scatter x1, waiting for transfers between devices, shards(): lax.psum_scatter(n_second, ('lat', 'lon'), scatter_dimension=0, tiled=True)  136 us
    reduce_scatter x1, waiting for transfers between devices, shards(): lax.psum_scatter(e_first, ('lat', 'lon'), scatter_dimension=0, tiled=True)  105 us
    unnamed x1, blocking collectives  40.7 us
    unnamed x91, local copies, waits for them, and re-layouts  40.3 us
    dot_general x5, matrix products, mlp_forward(): jnp.dot(piece, w_first[number * width:(number + 1) * width], preferred_el...  29.1 us
    reduce_scatter x1, waiting for transfers between devices, shards(): lax.psum_scatter(e_second, ('lat', 'lon'), scatter_dimension=0, tiled=True)  21 us
    gather x2, local copies, waits for them, and re-layouts, shards(): jnp.take(g_aggregate, rcv, axis=0)  19.5 us
  transfers between devices with their start and end apart: 15, of which 5 were waited for; matrix products, arithmetic and copies ran while one was open for 15% of the time, Pallas kernels for 0%

commit v1 on v0

--- a/solution.py
+++ b/solution.py
@@ -99,102 +99,156 @@
     node_n, width = nodes_l.shape
     halo_n = rows_out.shape[1]
     devices, slot_n = need.shape
-    sent = jnp.take(nodes_l, rows_out, axis=0)
+    axes = ("lat", "lon")
+
+    def exchange(value):
+        return lax.all_to_all(value, axes, split_axis=0, concat_axis=0, tiled=True)
+
+    def one_hot(ids, count, keep=None):
+        hit = ids[:, None] == jnp.arange(count)[None, :]
+        if keep is not None:
+            hit = hit & keep[:, None]
+        return hit.astype(jnp.bfloat16)
+
+    def one_hot_t(ids, count, keep=None):
+        hit = ids[None, :] == jnp.arange(count)[:, None]
+        if keep is not None:
+            hit = hit & keep[None, :]
+        return hit.astype(jnp.bfloat16)
+
+    def product(left, right):
+        return jnp.dot(left, right, preferred_element_type=jnp.float32)
+
+    sent = product(one_hot(rows_out.reshape(-1), node_n), nodes_l).astype(jnp.bfloat16)
+    sent = sent.reshape(4, halo_n, width)
     from_east = shifted(sent[0], "lon", 1)
     from_west = shifted(sent[1], "lon", -1)
     from_north = passed_along(sent[2], "lat", 1)
     from_south = passed_along(sent[3], "lat", -1)
-    wanted = lax.all_to_all(need, ("lat", "lon"), split_axis=0, concat_axis=0, tiled=True)
-    outgoing = jnp.take(nodes_l, wanted, axis=0)
-    far = lax.all_to_all(outgoing, ("lat", "lon"), split_axis=0, concat_axis=0, tiled=True).reshape(
-        devices * slot_n, width
-    )
+    coarse = exchange(jnp.broadcast_to(nodes_l[:COARSE][None], (devices, COARSE, width)))
+    far = jnp.zeros((devices, slot_n, width), jnp.bfloat16)
+    for c in range(COARSE):
+        far = jnp.where((need == c)[:, :, None], coarse[:, c][:, None, :], far)
+    far = far.reshape(devices * slot_n, width)
     table = jnp.concatenate([nodes_l, from_east, from_west, from_north, from_south, far], axis=0)
-    recv_rows = jnp.take(nodes_l, rcv, axis=0)
-    sent_rows = jnp.take(table, snd, axis=0)
-    edge_parts = (edges_l, sent_rows, recv_rows)
-    edge_out, edge_saved = mlp_forward(edge_parts, e_w1, e_b1, e_w2, e_gain)
+    table_n = table.shape[0]
+    w_edge, w_send, w_recv = (e_w1[i * width : (i + 1) * width] for i in range(3))
     alive = jnp.arange(edges_l.shape[0]) < count
     live = alive.astype(jnp.float32)[:, None]
+    z_edge = product(edges_l, w_edge) + e_b1
+    p_recv = product(nodes_l, w_recv).astype(jnp.bfloat16)
+    p_send = product(table, w_send).astype(jnp.bfloat16)
+    picked = jnp.concatenate([p_send, p_recv], axis=0)
+    columns = jnp.arange(table_n + node_n)[None, :]
+    pick = (
+        ((snd[:, None] == columns) | (rcv[:, None] + table_n == columns)) & alive[:, None]
+    ).astype(jnp.bfloat16)
+    z_first = z_edge + product(pick, picked)
+    active = jax.nn.silu(z_first).astype(jnp.bfloat16)
+    z_second = product(active, e_w2)
+    edge_out, normed, rstd = layer_norm(z_second, e_gain)
     new_edges = (edges_l + live * edge_out).astype(jnp.bfloat16)
-    recv_table = ((rcv[None, :] == jnp.arange(node_n)[:, None]) & alive[None, :]).astype(
-        jnp.bfloat16
-    )
-    aggregate = jnp.dot(recv_table, new_edges, preferred_element_type=jnp.float32).astype(
-        jnp.bfloat16
-    )
+    recv_t = one_hot_t(rcv, node_n, alive)
+    aggregate = product(recv_t, new_edges).astype(jnp.bfloat16)
     node_parts = (nodes_l, aggregate)
     node_out, node_saved = mlp_forward(node_parts, n_w1, n_b1, n_w2, n_gain)
     new_nodes = (nodes_l + node_out).astype(jnp.bfloat16)
     node_up = node_cot[0, 0].astype(jnp.float32)
     g_node_in, node_grads = mlp_backward(node_parts, node_saved, node_up, n_w1, n_w2, n_gain)
     n_first, n_bias, n_second, n_scale = node_grads
-    node_sums = (
-        lax.psum_scatter(n_first, ("lat", "lon"), scatter_dimension=0, tiled=True),
-        lax.psum_scatter(n_bias, ("lat", "lon"), scatter_dimension=0, tiled=True),
-        lax.psum_scatter(n_second, ("lat", "lon"), scatter_dimension=0, tiled=True),
-        lax.psum_scatter(n_scale, ("lat", "lon"), scatter_dimension=0, tiled=True),
-    )
-    g_aggregate = g_node_in[:, width:]
-    g_new_edges = edge_cot[0, 0].astype(jnp.float32) + live * jnp.take(g_aggregate, rcv, axis=0)
-    g_edge_in, edge_grads = mlp_backward(
-        edge_parts, edge_saved, live * g_new_edges, e_w1, e_w2, e_gain
-    )
-    e_first, e_bias, e_second, e_scale = edge_grads
-    g_edge_in = g_edge_in.astype(jnp.bfloat16)
-    edge_grad = g_new_edges + g_edge_in[:, :width]
-    send_table = (snd[None, :] == jnp.arange(table.shape[0])[:, None]).astype(jnp.bfloat16)
-    sender_grad = jnp.dot(
-        send_table, g_edge_in[:, width : 2 * width], preferred_element_type=jnp.float32
-    )
-    halo_part = sender_grad[node_n : node_n + 4 * halo_n]
-    to_east = shifted(halo_part[:halo_n].astype(jnp.bfloat16), "lon", -1).astype(jnp.float32)
-    to_west = shifted(halo_part[halo_n : 2 * halo_n].astype(jnp.bfloat16), "lon", 1).astype(
-        jnp.float32
-    )
-    to_north = passed_along(
-        halo_part[2 * halo_n : 3 * halo_n].astype(jnp.bfloat16), "lat", -1
+    g_aggregate = g_node_in[:, width:].astype(jnp.bfloat16)
+    g_new_edges = edge_cot[0, 0].astype(jnp.float32) + product(
+        one_hot(rcv, node_n, alive), g_aggregate
+    )
+    grad_out = live * g_new_edges
+    e_scale = jnp.sum(grad_out * normed, axis=0)
+    scaled = grad_out * e_gain
+    g_second = rstd * (
+        scaled
+        - jnp.mean(scaled, axis=-1, keepdims=True)
+        - normed * jnp.mean(scaled * normed, axis=-1, keepdims=True)
+    )
+    g_second = g_second.astype(jnp.bfloat16)
+    e_second = transposed(active, g_second)
+
+    def split(value):
+        return value.astype(jnp.bfloat16).reshape(devices, -1, value.shape[-1])
+
+    early = exchange(jnp.concatenate([split(n_first), split(n_second), split(e_second)], axis=1))
+    g_active = product(g_second, e_w2.T)
+    sigma = jax.nn.sigmoid(z_first)
+    g_first = (g_active * sigma * (1.0 + z_first * (1.0 - sigma))).astype(jnp.bfloat16)
+    e_bias = jnp.sum(g_first, axis=0, dtype=jnp.float32)
+    rows = jnp.arange(table_n + node_n)[:, None]
+    pick_t = (
+        ((snd[None, :] == rows) | (rcv[None, :] + table_n == rows)) & alive[None, :]
+    ).astype(jnp.bfloat16)
+    spread = product(pick_t, g_first).astype(jnp.bfloat16)
+    spread_send, spread_recv = spread[:table_n], spread[table_n:]
+    e_first = jnp.concatenate(
+        [
+            transposed(edges_l, g_first),
+            transposed(table, spread_send),
+            transposed(nodes_l, spread_recv),
+        ],
+        axis=0,
+    )
+    late = exchange(split(e_first))
+    sender_grad = product(spread_send, w_send.T)
+    edge_grad = g_new_edges + product(g_first, w_edge.T)
+    halo_part = sender_grad[node_n : node_n + 4 * halo_n].astype(jnp.bfloat16)
+    to_east = shifted(halo_part[:halo_n], "lon", -1)
+    to_west = shifted(halo_part[halo_n : 2 * halo_n], "lon", 1)
+    to_north = passed_along(halo_part[2 * halo_n : 3 * halo_n], "lat", -1)
+    to_south = passed_along(halo_part[3 * halo_n :], "lat", 1)
+    far_grad = sender_grad[node_n + 4 * halo_n :].reshape(devices, slot_n, width)
+    to_coarse = jnp.stack(
+        [
+            jnp.sum(jnp.where((need == c)[:, :, None], far_grad, 0.0), axis=1)
+            for c in range(COARSE)
+        ],
+        axis=1,
+    ).astype(jnp.bfloat16)
+    vectors = jnp.concatenate(
+        [v.reshape(devices, -1) for v in (e_bias, e_scale, n_bias, n_scale)], axis=1
+    )
+    high = vectors.astype(jnp.bfloat16)
+    low = (vectors - high.astype(jnp.float32)).astype(jnp.bfloat16)
+    extra = jnp.concatenate([high, low], axis=1)
+    vector_n = vectors.shape[1]
+    extra_rows = -(-extra.shape[1] // width)
+    extra = jnp.pad(extra, ((0, 0), (0, extra_rows * width - extra.shape[1])))
+    came = exchange(
+        jnp.concatenate([to_coarse, extra.reshape(devices, extra_rows, width)], axis=1)
     ).astype(jnp.float32)
-    to_south = passed_along(halo_part[3 * halo_n :].astype(jnp.bfloat16), "lat", 1).astype(
-        jnp.float32
-    )
-    far_grad = sender_grad[node_n + 4 * halo_n :]
-    came = (
-        lax.all_to_all(
-            far_grad.reshape(devices, slot_n, width).astype(jnp.bfloat16),
-            ("lat", "lon"),
-            split_axis=0,
-            concat_axis=0,
-            tiled=True,
-        )
-        .astype(jnp.float32)
-        .reshape(devices * slot_n, width)
-    )
-    coarse_table = (wanted.reshape(-1)[None, :] == jnp.arange(COARSE)[:, None]).astype(jnp.float32)
-    coarse_grad = jnp.dot(
-        coarse_table, came, precision=lax.Precision.HIGHEST, preferred_element_type=jnp.float32
-    )
+    came = jnp.sum(came, axis=0)
+    coarse_grad = came[:COARSE]
+    flat = came[COARSE:].reshape(-1)
+    vector = (flat[:vector_n] + flat[vector_n : 2 * vector_n]).reshape(4, -1)
     returned = jnp.concatenate([to_east, to_west, to_north, to_south], axis=0)
-    border_table = (rows_out.reshape(-1)[None, :] == jnp.arange(node_n)[:, None]).astype(
-        jnp.float32
-    )
+    border_t = one_hot_t(rows_out.reshape(-1), node_n)
     node_grad = (
         node_up
         + g_node_in[:, :width]
-        + jnp.dot(recv_table, g_edge_in[:, 2 * width :], preferred_element_type=jnp.float32)
-    )
-    node_grad = node_grad + sender_grad[:node_n]
-    node_grad = node_grad + jnp.dot(
-        border_table, returned, precision=lax.Precision.HIGHEST, preferred_element_type=jnp.float32
+        + product(spread_recv, w_recv.T)
+        + sender_grad[:node_n]
+        + product(border_t, returned)
     )
     node_grad = node_grad + jnp.pad(coarse_grad, ((0, node_n - COARSE), (0, 0)))
-    edge_sums = (
-        lax.psum_scatter(e_first, ("lat", "lon"), scatter_dimension=0, tiled=True),
-        lax.psum_scatter(e_bias, ("lat", "lon"), scatter_dimension=0, tiled=True),
-        lax.psum_scatter(e_second, ("lat", "lon"), scatter_dimension=0, tiled=True),
-        lax.psum_scatter(e_scale, ("lat", "lon"), scatter_dimension=0, tiled=True),
-    )
-    sums = edge_sums + node_sums
+    early = jnp.sum(early.astype(jnp.float32), axis=0)
+    late = jnp.sum(late.astype(jnp.float32), axis=0)
+    n_one = n_first.shape[0] // devices
+    n_two = n_one + n_second.shape[0] // devices
+    sums = (
+        late,
+        vector[0],
+        early[n_two:],
+        vector[1],
+        early[:n_one],
+        vector[2],
+        early[n_one:n_two],
+        vector[3],
+    )
     return (
         new_nodes[None, None],
         new_edges[None, None],

time: 699 us -> 194 us (0.28)
  waiting for transfers between devices: 404 us -> 53.2 us
  local copies, waits for them, and re-layouts: 100 us -> 35.3 us
  blocking collectives: 40.7 us -> 0 us
  other arithmetic: 35.4 us -> 13.4 us
  matrix products: 67.9 us -> 52.9 us
  between operations: 15.5 us -> 2.09 us
    reduce_scatter x4 -> x0, waiting for transfers between devices: 400 us -> none  [the longest x1 138 us: shards(): lax.psum_scatter(n_first, ('lat', 'lon'), scatter_dimension=0, tiled=True)]
    gather x8 -> x0, local copies, waits for them, and re-layouts: 56.8 us -> none  [the longest x2 19.5 us: shards(): jnp.take(g_aggregate, rcv, axis=0)]
    unnamed x1 -> x0, blocking collectives: 40.7 us -> none
    all_to_all x3 -> x4, waiting for transfers between devices: 4.16 us -> 43.8 us  [exchange(): return lax.all_to_all(value, axes, split_axis=0, concat_axis=0, tiled=True)]
    dot_general x5 -> x14, matrix products: 10.3 us -> 42.6 us  [product(): return jnp.dot(left, right, preferred_element_type=jnp.float32)]
    dot_general x5 -> x2, matrix products: 29.1 us -> 0.73 us  [mlp_forward(): jnp.dot(piece, w_first[number * width:(number + 1) * width], preferred_el...]
    unnamed x91 -> x99, local copies, waits for them, and re-layouts: 40.3 us -> 29.1 us
    ppermute x4, waiting for transfers between devices: 0.01 us -> 9.44 us  [shifted(): return lax.ppermute(block, axis, route)]
  transfers between devices with their start and end apart: 15 -> 12, of which waited for: 5 -> 5; matrix products, arithmetic and copies ran while one was open for 15% -> 26% of each run, Pallas kernels for 0% -> 0%
where the time goes in v1:
time: 194 us; the launch traced here: 193 us
  waiting for transfers between devices  53.2 us (27%)
  matrix products  52.9 us (27%)
  starting transfers between devices  35.6 us (18%)
  local copies, waits for them, and re-layouts  35.3 us (18%)
  other arithmetic  13.4 us (7%)
  between operations  2.09 us (1%)
    all_to_all x4, waiting for transfers between devices, exchange(): return lax.all_to_all(value, axes, split_axis=0, concat_axis=0, tiled=True)  43.8 us
    dot_general x14, matrix products, product(): return jnp.dot(left, right, preferred_element_type=jnp.float32)  42.6 us
    unnamed x99, local copies, waits for them, and re-layouts  29.1 us
    all_to_all x4, starting transfers between devices, exchange(): return lax.all_to_all(value, axes, split_axis=0, concat_axis=0, tiled=True)  19 us
    ppermute x4, waiting for transfers between devices, shifted(): return lax.ppermute(block, axis, route)  9.44 us
    ppermute x4, starting transfers between devices, shifted(): return lax.ppermute(block, axis, route)  9.26 us
    dot_general x7, matrix products, transposed(): lax.dot_general(left, right, (((0,), (0,)), ((), ())), preferred_element_...  7.99 us
    ppermute x4, starting transfers between devices, passed_along(): lax.ppermute(value, axis, [(source, source + steps) for source in range(l...  7.35 us
  transfers between devices with their start and end apart: 12, of which 5 were waited for; matrix products, arithmetic and copies ran while one was open for 26% of the time, Pallas kernels for 0%

profile of v1, /device:TPU:0, one launch (start us, length us, event | category | flops | bytes accessed | tf_op | source)
XLA Modules:
  0.0 192.5 jit_solution(3141281326137853703)
XLA Ops:
  0.7 0.8 slice_bitcast_fusion
  1.5 0.7 broadcast_in_dim.47
  2.2 7.3 %all-to-all-start = ((bf16[32,2,512]{2,1,0:T(2,128)(2,1)}), bf16[32,2,512]{2,1,0:T(2,128)(2,1)S(1)}, u32[]{:S(2)}, u32[]{:S(2)}) async-start(bf16[32,2,512]{2,1,0:T(2,128)(2,1)} %broadcast_in_dim.47), calls=%async_computation | async-start | bytes 131072 | tf_op jit(solution)/shard_map/all_to_all | solution.py:105
  9.5 0.8 eq.147
  10.3 1.2 convolution_convert_fusion.8
  11.6 1.3 collective-permute-start.3
  12.9 3.0 %collective-permute-start.2 = (bf16[24,512]{1,0:T(8,128)(2,1)S(1)}, bf16[24,512]{1,0:T(8,128)(2,1)S(1)}, u32[]{:S(2)}, u32[]{:S(2)}) collective-permute-start(bf16[24,512]{1,0:T(8,128)(2,1)S(1)} %get-tuple-element.67), channel_id=1, source_target_pairs={{0,8},{8,16},{16,24},{1,9},{9,17},{17,25},{2,10},{10,18},{18,26},{... | collective-permute-start | bytes 73736 | tf_op jit(solution)/shard_map/ppermute | solution.py:21
  15.9 4.6 %collective-permute-start.1 = (bf16[24,512]{1,0:T(8,128)(2,1)S(1)}, bf16[24,512]{1,0:T(8,128)(2,1)S(1)}, u32[]{:S(2)}, u32[]{:S(2)}) collective-permute-start(bf16[24,512]{1,0:T(8,128)(2,1)S(1)} %get-tuple-element.68), channel_id=1, source_target_pairs={{1,0},{2,1},{3,2},{4,3},{5,4},{6,5},{7,6},{0,7},{9,8},{10,9},{11,1... | collective-permute-start | bytes 73736 | tf_op jit(solution)/shard_map/ppermute | solution.py:15
  20.5 1.0 bitcast_dynamic-update-slice_fusion
  22.2 0.7 compare_bitcast_fusion.1
  22.9 0.7 broadcast_add_fusion
  23.6 2.3 %convolution_convert_fusion.7 = bf16[384,512]{1,0:T(8,128)(2,1)} fusion(bf16[1536,512]{1,0:T(8,128)(2,1)} %param.26, bf16[1,1,384,512]{3,2,1,0:T(8,128)(2,1)} %param.17), kind=kOutput, calls=%fused_computation.67 | convolution fusion | flops 201523200 | bytes 1310720 | tf_op jit(solution)/shard_map/dot_general | solution.py:120
  26.3 4.6 %copy.42 = bf16[1,1,3072,512]{2,3,1,0:T(8,128)(2,1)} copy(bf16[1,1,3072,512]{3,2,1,0:T(8,128)(2,1)} %param.25) | data formatting | bytes 6291456 | tf_op args[8]
  30.9 4.6 %copy.39 = bf16[1,1,3072,512]{2,3,1,0:T(8,128)(2,1)} copy(bf16[1,1,3072,512]{3,2,1,0:T(8,128)(2,1)} %param.18) | data formatting | bytes 6291456 | tf_op args[1]
  35.5 0.7 constant_dynamic-update-slice_fusion.3
  36.6 1.7 convolution_convert_fusion.6
  38.3 5.4 %fusion.2 = f32[3072,512]{1,0:T(8,128)S(1)} fusion(s32[3072]{0:T(1024)S(1)} %broadcast_add_fusion, s32[3072]{0:T(1024)} %bitcast.112, pred[3072]{0:T(1024)(128)(4,1)S(1)} %get-tuple-element.91, bf16[384,512]{1,0:T(8,128)(2,1)} %convolution_convert_fusion.7, bf16[512,512]{1,0:T(8,128)(2,1)S(1)} %convolution_convert_fusion.6), kind=kOutput, calls=%fused_computation.6 | convolution fusion | flops 2831417344 | bytes 7236608 | tf_op jit(solution)/shard_map/dot_general | solution.py:120
  43.7 4.0 %multiply_convert_fusion.2 = (bf16[3072,512]{1,0:T(8,128)(2,1)S(1)}, f32[3072,512]{1,0:T(8,128)}) fusion(f32[3072,512]{1,0:T(8,128)S(1)} %fusion.2, f32[512]{0:T(512)S(1)} %copy-done.42, bf16[1536,512]{1,0:T(8,128)(2,1)S(1)} %copy-done.20, bf16[1,1,3072,512]{3,2,1,0:T(8,128)(2,1)S(1)} %copy-done.17), kind=kOutput, calls=%fused_computation.19 | convolution fusion | flops 1621622784 | bytes 19400704 | tf_op jit(solution)/shard_map/dot_general | solution.py:120
  47.8 1.9 %fusion.102 = (f32[3072]{0:T(1024)S(1)}, f32[3072,512]{0,1:T(8,128)S(1)}) fusion(bf16[3072,512]{1,0:T(8,128)(2,1)S(1)} %get-tuple-element.78, bf16[512,512]{1,0:T(8,128)(2,1)S(1)} %copy-done), kind=kOutput, calls=%fused_computation.172 | convolution fusion | flops 1612182528 | bytes 9973760 | tf_op jit(solution)/shard_map/dot_general | solution.py:120
  49.8 0.8 multiply_reduce_fusion.2
  50.6 1.1 copy-done.5
  51.6 1.8 add_convert_fusion
  53.4 1.4 fusion.38
  57.3 1.1 fusion.54
  58.4 0.6 convert_reduce_fusion.3
  59.0 0.6 fusion.105
  59.6 0.8 copy-done.18
  60.4 4.3 %multiply_reduce_fusion = (f32[512]{0:T(512)S(1)}, f32[3072]{0:T(1024)S(1)}, f32[3072]{0:T(1024)S(1)}, f32[3072,512]{0,1:T(8,128)S(1)}) fusion(f32[3072,512]{0,1:T(8,128)S(1)} %get-tuple-element.81, f32[3072]{0:T(1024)S(1)} %add_rsqrt_fusion, f32[3072]{0:T(1024)S(1)} %broadcast_multiply_fusion.2, f32[3072]{0:T(1024)S(1)} %get-tuple-element.92, ...), kind=kOutput, calls=%fused_computation.12 | convolution fusion | flops 1227613696 | bytes 16202752 | tf_op jit(solution)/shard_map/dot_general | solution.py:120
  64.8 2.1 %multiply_convert_fusion.1 = bf16[3072,512]{0,1:T(8,128)(2,1)S(1)} fusion(f32[3072,512]{0,1:T(8,128)S(1)} %get-tuple-element.84, f32[3072,512]{0,1:T(8,128)S(1)} %get-tuple-element.81, f32[3072]{0:T(1024)S(1)} %broadcast_multiply_fusion, f32[3072]{0:T(1024)S(1)} %broadcast_multiply_fusion.1, f32[512]{0:T(512)S(1)} %copy-done.29, f32[3072]{0:T(1024)S(1)} %add_rsqrt_fusion, ...), kind=kLoop, calls=%fused_computation.15 | loop fusion | flops 14155776 | bytes 15792128 | tf_op jit(solution)/shard_map/convert_element_type | solution.py:171
  66.9 0.5 copy-done.2
  67.4 4.3 %convert_reduce_fusion = (f32[512]{0:T(512)S(1)}, bf16[3072,512]{1,0:T(8,128)(2,1)S(1)}) fusion(f32[3072,512]{1,0:T(8,128)S(1)} %bitcast.115, bf16[3072,512]{0,1:T(8,128)(2,1)S(1)} %multiply_convert_fusion.1, bf16[512,512]{1,0:T(8,128)(2,1)S(1)} %copy-done), kind=kOutput, calls=%fused_computation.13 | convolution fusion | flops 1627913728 | bytes 13109248 | tf_op jit(solution)/shard_map/dot_general | solution.py:120
  71.8 1.8 fusion.41
  73.7 3.0 %fusion.27 = bf16[896,512]{1,0:T(8,128)(2,1)S(1)} fusion(bf16[3072,512]{1,0:T(8,128)(2,1)S(1)} %get-tuple-element.88, s32[3072]{0:T(1024)S(1)} %broadcast_add_fusion, s32[3072]{0:T(1024)S(1)} %bitcast.113, pred[3072]{0:T(1024)(128)(4,1)S(1)} %copy-done.34), kind=kOutput, calls=%fused_computation.47 | convolution fusion | flops 2830041088 | bytes 4090880 | tf_op jit(solution)/shard_map/dot_general | solution.py:120
  76.7 1.3 convolution_convert_fusion.5
  78.5 1.3 fusion.104
  80.4 0.8 copy.43
  81.2 6.0 %all-to-all-start.1 = ((bf16[32,3,512]{2,1,0:T(4,128)(2,1)}), bf16[32,3,512]{2,1,0:T(4,128)(2,1)S(1)}, u32[]{:S(2)}, u32[]{:S(2)}) async-start(bf16[32,3,512]{2,1,0:T(4,128)(2,1)} %copy.43), calls=%async_computation.1 | async-start | bytes 262144 | tf_op jit(solution)/shard_map/all_to_all | solution.py:105
  87.2 2.3 %pad_maximum_fusion.1 = bf16[1536,512]{1,0:T(8,128)(2,1)} fusion(bf16[512,512]{1,0:T(8,128)(2,1)S(1)} %fusion.44, bf16[512,512]{1,0:T(8,128)(2,1)} %convolution_convert_fusion.5, bf16[512,512]{1,0:T(8,128)(2,1)S(1)} %fusion.41), kind=kLoop, calls=%fused_computation.46 | loop fusion | flops 4718592 | bytes 3145728 | tf_op jit(solution)/shard_map/concatenate | solution.py:188
  89.5 5.5 %all-to-all-done.1 = bf16[32,3,512]{2,1,0:T(4,128)(2,1)S(1)} async-done(((bf16[32,3,512]{2,1,0:T(4,128)(2,1)}), bf16[32,3,512]{2,1,0:T(4,128)(2,1)S(1)}, u32[]{:S(2)}, u32[]{:S(2)}) %all-to-all-start.1) | async-done | bytes 98336 | tf_op jit(solution)/shard_map/all_to_all | solution.py:105
  95.0 2.9 %all-to-all-start.2 = ((bf16[32,48,512]{2,1,0:T(8,128)(2,1)}), bf16[32,48,512]{2,1,0:T(8,128)(2,1)S(1)}, u32[]{:S(2)}, u32[]{:S(2)}) async-start(bf16[32,48,512]{2,1,0:T(8,128)(2,1)} %bitcast.105), calls=%async_computation.2 | async-start | bytes 3145728 | tf_op jit(solution)/shard_map/all_to_all | solution.py:105
  98.0 1.5 convolution_convert_fusion.2
  100.6 1.3 copy-done.8
  101.9 1.0 copy-done.16
  102.8 1.9 convolution_convert_fusion
  104.7 1.5 pad_maximum_fusion
  106.3 30.2 %all-to-all-done.2 = bf16[32,48,512]{2,1,0:T(8,128)(2,1)S(1)} async-done(((bf16[32,48,512]{2,1,0:T(8,128)(2,1)}), bf16[32,48,512]{2,1,0:T(8,128)(2,1)S(1)}, u32[]{:S(2)}, u32[]{:S(2)}) %all-to-all-start.2) | async-done | bytes 1572896 | tf_op jit(solution)/shard_map/all_to_all | solution.py:105
  136.5 1.2 copy-done.9
  137.6 2.7 %all-to-all-start.3 = ((bf16[32,64,512]{2,1,0:T(8,128)(2,1)}), bf16[32,64,512]{2,1,0:T(8,128)(2,1)S(1)}, u32[]{:S(2)}, u32[]{:S(2)}) async-start(bf16[32,64,512]{2,1,0:T(8,128)(2,1)} %pad_maximum_fusion), calls=%async_computation.3 | async-start | bytes 4194304 | tf_op jit(solution)/shard_map/all_to_all | solution.py:105
  140.4 4.6 %copy.45 = bf16[1,1,3072,512]{3,2,1,0:T(8,128)(2,1)} copy(bf16[1,1,3072,512]{2,3,1,0:T(8,128)(2,1)} %bitcast.104) | data formatting | bytes 6291456
  145.0 8.4 %add_bitcast_fusion = f32[1,1,3072,512]{2,3,1,0:T(8,128)} fusion(f32[3072,512]{0,1:T(8,128)} %copy-done.2, bf16[3072,512]{1,0:T(8,128)(2,1)} %copy-done.6, bf16[1536,512]{1,0:T(8,128)(2,1)} %param.26), kind=kOutput, calls=%fused_computation.11 | convolution fusion | flops 1612185600 | bytes 16252928 | tf_op jit(solution)/shard_map/dot_general | solution.py:120
  153.4 6.6 %copy.46 = f32[1,1,3072,512]{3,2,1,0:T(8,128)} copy(f32[1,1,3072,512]{2,3,1,0:T(8,128)} %add_bitcast_fusion) | data formatting | bytes 12582912
  160.0 0.9 fusion.98
  160.9 4.6 %collective-permute-start.4 = (bf16[24,512]{1,0:T(8,128)(2,1)S(1)}, bf16[24,512]{1,0:T(8,128)(2,1)S(1)}, u32[]{:S(2)}, u32[]{:S(2)}) collective-permute-start(bf16[24,512]{1,0:T(8,128)(2,1)S(1)} %get-tuple-element.60), channel_id=1, source_target_pairs={{1,0},{2,1},{3,2},{4,3},{5,4},{6,5},{7,6},{0,7},{9,8},{10,9},{11,1... | collective-permute-start | bytes 73736 | tf_op jit(solution)/shard_map/ppermute | solution.py:15
  165.5 1.7 collective-permute-start.7
  167.2 1.3 collective-permute-start.6
  168.6 2.1 %fusion.34 = f32[384,512]{1,0:T(8,128)S(1)} fusion(f32[512,512]{1,0:T(8,128)} %copy-done.14, f32[384,1024]{1,0:T(8,128)} %copy-done.12, bf16[1536,512]{1,0:T(8,128)(2,1)} %param.26, bf16[1,1,384,512]{3,2,1,0:T(8,128)(2,1)S(1)} %copy-done.13, bf16[896,512]{1,0:T(8,128)(2,1)} %copy-done.19), kind=kOutput, calls=%fused_computation.61 | convolution fusion | flops 202113024 | bytes 3670016 | tf_op jit(solution)/shard_map/dot_general | solution.py:120
  170.8 4.6 %collective-permute-done.4 = bf16[24,512]{1,0:T(8,128)(2,1)S(1)} collective-permute-done((bf16[24,512]{1,0:T(8,128)(2,1)S(1)}, bf16[24,512]{1,0:T(8,128)(2,1)S(1)}, u32[]{:S(2)}, u32[]{:S(2)}) %collective-permute-start.4) | collective-permute-done | bytes 24608 | tf_op jit(solution)/shard_map/ppermute | solution.py:15
  175.3 4.9 %collective-permute-done.5 = bf16[24,512]{1,0:T(8,128)(2,1)S(1)} collective-permute-done((bf16[24,512]{1,0:T(8,128)(2,1)S(1)}, bf16[24,512]{1,0:T(8,128)(2,1)S(1)}, u32[]{:S(2)}, u32[]{:S(2)}) %collective-permute-start.5) | collective-permute-done | bytes 24608 | tf_op jit(solution)/shard_map/ppermute | solution.py:15
  180.2 1.1 fusion.36
  181.4 0.6 slice_bitcast_fusion.1
  182.0 0.9 convert_reduce_fusion.2
  182.9 8.0 %all-to-all-done.3 = bf16[32,64,512]{2,1,0:T(8,128)(2,1)S(1)} async-done(((bf16[32,64,512]{2,1,0:T(8,128)(2,1)}), bf16[32,64,512]{2,1,0:T(8,128)(2,1)S(1)}, u32[]{:S(2)}, u32[]{:S(2)}) %all-to-all-start.3) | async-done | bytes 2097184 | tf_op jit(solution)/shard_map/all_to_all | solution.py:105
  191.3 0.6 slice.185
  191.9 0.6 fusion.99
  (130 shorter events, 5.8 us)
Async XLA Ops:
  0.6 47.1 %copy-start = (bf16[512,512]{1,0:T(8,128)(2,1)S(1)}, bf16[512,512]{1,0:T(8,128)(2,1)}, u32[]{:S(2)}) copy-start(bf16[512,512]{1,0:T(8,128)(2,1)} %param.28) | copy-start | bytes 1572868
  0.7 25.2 %copy-start.3 = (bf16[1,1,384,512]{3,2,1,0:T(8,128)(2,1)S(1)}, bf16[1,1,384,512]{3,2,1,0:T(8,128)(2,1)}, u32[]{:S(2)}) copy-start(bf16[1,1,384,512]{3,2,1,0:T(8,128)(2,1)} %param.17) | copy-start | bytes 1179652
  0.7 25.2 %copy-start.11 = (bf16[1024,512]{1,0:T(8,128)(2,1)S(1)}, bf16[1024,512]{1,0:T(8,128)(2,1)}, u32[]{:S(2)}) copy-start(bf16[1024,512]{1,0:T(8,128)(2,1)} %param.30) | copy-start | bytes 3145732
  0.7 25.2 %copy-start.35 = (f32[512]{0:T(512)S(1)}, f32[512]{0:T(512)}, u32[]{:S(2)}) copy-start(f32[512]{0:T(512)} %param.31) | copy-start | bytes 6148
  2.2 34.1 %all-to-all-start = ((bf16[32,2,512]{2,1,0:T(2,128)(2,1)}), bf16[32,2,512]{2,1,0:T(2,128)(2,1)S(1)}, u32[]{:S(2)}, u32[]{:S(2)}) async-start(bf16[32,2,512]{2,1,0:T(2,128)(2,1)} %broadcast_in_dim.47), calls=%async_computation | async-start | bytes 131072 | tf_op jit(solution)/shard_map/all_to_all | solution.py:105
  10.3 13.3 %copy-start.31 = (s32[96]{0:T(128)}, s32[96]{0:T(128)S(1)}, u32[]{:S(2)}) copy-start(s32[96]{0:T(128)S(1)} %eq.147) | copy-start | bytes 1156
  11.6 24.7 %collective-permute-start.3 = (bf16[24,512]{1,0:T(8,128)(2,1)S(1)}, bf16[24,512]{1,0:T(8,128)(2,1)S(1)}, u32[]{:S(2)}, u32[]{:S(2)}) collective-permute-start(bf16[24,512]{1,0:T(8,128)(2,1)S(1)} %get-tuple-element.66), channel_id=1, source_target_pairs={{8,0},{16,8},{24,16},{9,1},{17,9},{25,17},{10,2},{18,10},{26,18},{... | collective-permute-start | bytes 73736 | tf_op jit(solution)/shard_map/ppermute | solution.py:21
  12.9 23.4 %collective-permute-start.2 = (bf16[24,512]{1,0:T(8,128)(2,1)S(1)}, bf16[24,512]{1,0:T(8,128)(2,1)S(1)}, u32[]{:S(2)}, u32[]{:S(2)}) collective-permute-start(bf16[24,512]{1,0:T(8,128)(2,1)S(1)} %get-tuple-element.67), channel_id=1, source_target_pairs={{0,8},{8,16},{16,24},{1,9},{9,17},{17,25},{2,10},{10,18},{18,26},{... | collective-permute-start | bytes 73736 | tf_op jit(solution)/shard_map/ppermute | solution.py:21
  15.9 20.4 %collective-permute-start.1 = (bf16[24,512]{1,0:T(8,128)(2,1)S(1)}, bf16[24,512]{1,0:T(8,128)(2,1)S(1)}, u32[]{:S(2)}, u32[]{:S(2)}) collective-permute-start(bf16[24,512]{1,0:T(8,128)(2,1)S(1)} %get-tuple-element.68), channel_id=1, source_target_pairs={{1,0},{2,1},{3,2},{4,3},{5,4},{6,5},{7,6},{0,7},{9,8},{10,9},{11,1... | collective-permute-start | bytes 73736 | tf_op jit(solution)/shard_map/ppermute | solution.py:15
  20.5 15.0 %collective-permute-start = (bf16[24,512]{1,0:T(8,128)(2,1)S(1)}, bf16[24,512]{1,0:T(8,128)(2,1)}, u32[]{:S(2)}, u32[]{:S(2)}) collective-permute-start(bf16[24,512]{1,0:T(8,128)(2,1)S(1)} %get-tuple-element.69), channel_id=1, source_target_pairs={{7,0},{0,1},{1,2},{2,3},{3,4},{4,5},{5,6},{6,7},{15,8},{8,9},{9,10... | collective-permute-start | bytes 73736 | tf_op jit(solution)/shard_map/ppermute | solution.py:15
  22.9 13.6 %copy-start.36 = (pred[32]{0:T(512)(128)(4,1)}, pred[32]{0:T(512)(128)(4,1)S(1)}, u32[]{:S(2)}) copy-start(pred[32]{0:T(512)(128)(4,1)S(1)} %get-tuple-element.76) | copy-start | bytes 100
  22.9 13.6 %copy-start.38 = (pred[32]{0:T(512)(128)(4,1)}, pred[32]{0:T(512)(128)(4,1)S(1)}, u32[]{:S(2)}) copy-start(pred[32]{0:T(512)(128)(4,1)S(1)} %get-tuple-element.77) | copy-start | bytes 100
  26.2 27.1 %copy-start.33 = (pred[3072]{0:T(1024)(128)(4,1)}, pred[3072]{0:T(1024)(128)(4,1)S(1)}, u32[]{:S(2)}) copy-start(pred[3072]{0:T(1024)(128)(4,1)S(1)} %get-tuple-element.91) | copy-start | bytes 9220
  36.5 7.2 %copy-start.26 = (bf16[512,512]{1,0:T(8,128)(2,1)}, bf16[512,512]{1,0:T(8,128)(2,1)S(1)}, u32[]{:S(2)}) copy-start(bf16[512,512]{1,0:T(8,128)(2,1)S(1)} %fusion.93) | copy-start | bytes 1572868
  38.2 5.5 %copy-start.17 = (bf16[1,1,3072,512]{3,2,1,0:T(8,128)(2,1)S(1)}, bf16[1,1,3072,512]{3,2,1,0:T(8,128)(2,1)}, u32[]{:S(2)}) copy-start(bf16[1,1,3072,512]{3,2,1,0:T(8,128)(2,1)} %param.18) | copy-start | bytes 9437188
  38.2 5.5 %copy-start.20 = (bf16[1536,512]{1,0:T(8,128)(2,1)S(1)}, bf16[1536,512]{1,0:T(8,128)(2,1)}, u32[]{:S(2)}) copy-start(bf16[1536,512]{1,0:T(8,128)(2,1)} %param.26) | copy-start | bytes 4718596
  38.3 5.5 %copy-start.42 = (f32[512]{0:T(512)S(1)}, f32[512]{0:T(512)}, u32[]{:S(2)}) copy-start(f32[512]{0:T(512)} %param.27) | copy-start | bytes 6148
  47.8 2.0 %copy-start.7 = (bf16[3072,512]{1,0:T(8,128)(2,1)}, bf16[3072,512]{1,0:T(8,128)(2,1)S(1)}, u32[]{:S(2)}) copy-start(bf16[3072,512]{1,0:T(8,128)(2,1)S(1)} %get-tuple-element.78) | copy-start | bytes 9437188
  49.7 1.9 copy-start.5
  49.8 1.9 copy-start.29
  51.6 1.8 copy-start.28
  53.4 1.7 copy-start.4
  53.4 2.1 %copy-start.40 = (bf16[512,512]{1,0:T(8,128)(2,1)S(1)}, bf16[512,512]{1,0:T(8,128)(2,1)}, u32[]{:S(2)}) copy-start(bf16[512,512]{1,0:T(8,128)(2,1)} %param.32) | copy-start | bytes 1572868
  55.1 0.9 copy-start.21
  55.5 2.9 %copy-start.22 = (f32[384,512]{1,0:T(8,128)}, f32[384,512]{1,0:T(8,128)S(1)}, u32[]{:S(2)}) copy-start(f32[384,512]{1,0:T(8,128)S(1)} %convolution_add_fusion.1) | copy-start | bytes 2359300
  55.5 1.3 copy-start.13
  55.5 1.3 copy-start.30
  58.4 1.2 copy-start.24
  58.4 2.0 %copy-start.18 = (bf16[1,1,3072,512]{2,3,1,0:T(8,128)(2,1)S(1)}, bf16[1,1,3072,512]{2,3,1,0:T(8,128)(2,1)}, u32[]{:S(2)}) copy-start(bf16[1,1,3072,512]{2,3,1,0:T(8,128)(2,1)} %copy.42) | copy-start | bytes 9437188
  58.4 2.0 %copy-start.34 = (pred[3072]{0:T(1024)(128)(4,1)S(1)}, pred[3072]{0:T(1024)(128)(4,1)}, u32[]{:S(2)}) copy-start(pred[3072]{0:T(1024)(128)(4,1)} %copy-done.33) | copy-start | bytes 9220
  59.0 8.5 %slice-start = ((s8[6291456]{0:T(1024)(128)(4,1)}), s8[4194304]{0:T(1024)(128)(4,1)S(1)}, s32[]{:S(2)}) async-start(s8[6291456]{0:T(1024)(128)(4,1)} %bitcast.114), calls=%async_computation.4 | async-start | bytes 8388608
  60.4 4.4 %copy-start.12 = (f32[384,1024]{1,0:T(8,128)}, f32[384,1024]{1,0:T(8,128)S(1)}, u32[]{:S(2)}) copy-start(f32[384,1024]{1,0:T(8,128)S(1)} %fusion.105) | copy-start | bytes 4718596
  60.4 7.0 %slice-start.1 = ((s8[6291456]{0:T(1024)(128)(4,1)}), s8[2097152]{0:T(1024)(128)(4,1)S(1)}, s32[]{:S(2)}) async-start(s8[6291456]{0:T(1024)(128)(4,1)} %bitcast.114), calls=%async_computation.5 | async-start | bytes 4194304
  64.8 2.6 %copy-start.2 = (f32[3072,512]{0,1:T(8,128)}, f32[3072,512]{0,1:T(8,128)S(1)}, u32[]{:S(2)}) copy-start(f32[3072,512]{0,1:T(8,128)S(1)} %get-tuple-element.84) | copy-start | bytes 18874372
  67.4 4.4 %copy-start.15 = (bf16[3072,512]{0,1:T(8,128)(2,1)}, bf16[3072,512]{0,1:T(8,128)(2,1)S(1)}, u32[]{:S(2)}) copy-start(bf16[3072,512]{0,1:T(8,128)(2,1)S(1)} %multiply_convert_fusion.1) | copy-start | bytes 9437188
  71.8 1.8 copy-start.6
  71.8 1.8 copy-start.41
  73.6 3.0 %copy-start.27 = (bf16[512,512]{1,0:T(8,128)(2,1)S(1)}, bf16[512,512]{1,0:T(8,128)(2,1)}, u32[]{:S(2)}) copy-start(bf16[512,512]{1,0:T(8,128)(2,1)} %copy-done.26) | copy-start | bytes 1572868
  76.7 1.8 copy-start.19
  76.7 3.4 %copy-start.37 = (pred[32]{0:T(512)(128)(4,1)S(1)}, pred[32]{0:T(512)(128)(4,1)}, u32[]{:S(2)}) copy-start(pred[32]{0:T(512)(128)(4,1)} %copy-done.36) | copy-start | bytes 100
  76.7 3.4 %copy-start.39 = (pred[32]{0:T(512)(128)(4,1)S(1)}, pred[32]{0:T(512)(128)(4,1)}, u32[]{:S(2)}) copy-start(pred[32]{0:T(512)(128)(4,1)} %copy-done.38) | copy-start | bytes 100
  79.8 15.2 %copy-start.14 = (f32[512,512]{1,0:T(8,128)}, f32[512,512]{1,0:T(8,128)S(1)}, u32[]{:S(2)}) copy-start(f32[512,512]{1,0:T(8,128)S(1)} %get-tuple-element.90) | copy-start | bytes 3145732
  81.2 13.8 %all-to-all-start.1 = ((bf16[32,3,512]{2,1,0:T(4,128)(2,1)}), bf16[32,3,512]{2,1,0:T(4,128)(2,1)S(1)}, u32[]{:S(2)}, u32[]{:S(2)}) async-start(bf16[32,3,512]{2,1,0:T(4,128)(2,1)} %copy.43), calls=%async_computation.1 | async-start | bytes 262144 | tf_op jit(solution)/shard_map/all_to_all | solution.py:105
  95.0 41.5 %all-to-all-start.2 = ((bf16[32,48,512]{2,1,0:T(8,128)(2,1)}), bf16[32,48,512]{2,1,0:T(8,128)(2,1)S(1)}, u32[]{:S(2)}, u32[]{:S(2)}) async-start(bf16[32,48,512]{2,1,0:T(8,128)(2,1)} %bitcast.105), calls=%async_computation.2 | async-start | bytes 3145728 | tf_op jit(solution)/shard_map/all_to_all | solution.py:105
  97.9 2.2 %copy-start.23 = (f32[384,512]{1,0:T(8,128)S(1)}, f32[384,512]{1,0:T(8,128)}, u32[]{:S(2)}) copy-start(f32[384,512]{1,0:T(8,128)} %copy-done.22) | copy-start | bytes 2359300
  97.9 2.2 %copy-start.25 = (bf16[384,512]{1,0:T(8,128)(2,1)S(1)}, bf16[384,512]{1,0:T(8,128)(2,1)}, u32[]{:S(2)}) copy-start(bf16[384,512]{1,0:T(8,128)(2,1)} %copy-done.24) | copy-start | bytes 1179652
  100.0 1.9 copy-start.8
  100.0 2.8 %copy-start.16 = (bf16[3072,512]{0,1:T(8,128)(2,1)S(1)}, bf16[3072,512]{0,1:T(8,128)(2,1)}, u32[]{:S(2)}) copy-start(bf16[3072,512]{0,1:T(8,128)(2,1)} %copy-done.15) | copy-start | bytes 9437188
  136.5 1.2 copy-start.9
  137.6 53.3 %all-to-all-start.3 = ((bf16[32,64,512]{2,1,0:T(8,128)(2,1)}), bf16[32,64,512]{2,1,0:T(8,128)(2,1)S(1)}, u32[]{:S(2)}, u32[]{:S(2)}) async-start(bf16[32,64,512]{2,1,0:T(8,128)(2,1)} %pad_maximum_fusion), calls=%async_computation.3 | async-start | bytes 4194304 | tf_op jit(solution)/shard_map/all_to_all | solution.py:105
  160.0 20.3 %copy-start.32 = (s32[96]{0:T(128)S(1)}, s32[96]{0:T(128)}, u32[]{:S(2)}) copy-start(s32[96]{0:T(128)} %copy-done.31) | copy-start | bytes 1156
  160.0 22.1 %copy-start.10 = (bf16[32,48,512]{2,1,0:T(8,128)(2,1)S(1)}, bf16[32,48,512]{2,1,0:T(8,128)(2,1)}, u32[]{:S(2)}) copy-start(bf16[32,48,512]{2,1,0:T(8,128)(2,1)} %copy-done.9) | copy-start | bytes 4718596
  160.9 14.5 %collective-permute-start.4 = (bf16[24,512]{1,0:T(8,128)(2,1)S(1)}, bf16[24,512]{1,0:T(8,128)(2,1)S(1)}, u32[]{:S(2)}, u32[]{:S(2)}) collective-permute-start(bf16[24,512]{1,0:T(8,128)(2,1)S(1)} %get-tuple-element.60), channel_id=1, source_target_pairs={{1,0},{2,1},{3,2},{4,3},{5,4},{6,5},{7,6},{0,7},{9,8},{10,9},{11,1... | collective-permute-start | bytes 73736 | tf_op jit(solution)/shard_map/ppermute | solution.py:15
  165.5 9.9 %collective-permute-start.7 = (bf16[24,512]{1,0:T(8,128)(2,1)S(1)}, bf16[24,512]{1,0:T(8,128)(2,1)S(1)}, u32[]{:S(2)}, u32[]{:S(2)}) collective-permute-start(bf16[24,512]{1,0:T(8,128)(2,1)S(1)} %get-tuple-element.61), channel_id=1, source_target_pairs={{0,8},{8,16},{16,24},{1,9},{9,17},{17,25},{2,10},{10,18},{18,26},{... | collective-permute-start | bytes 73736 | tf_op jit(solution)/shard_map/ppermute | solution.py:21
  167.2 8.1 %collective-permute-start.6 = (bf16[24,512]{1,0:T(8,128)(2,1)S(1)}, bf16[24,512]{1,0:T(8,128)(2,1)S(1)}, u32[]{:S(2)}, u32[]{:S(2)}) collective-permute-start(bf16[24,512]{1,0:T(8,128)(2,1)S(1)} %get-tuple-element.62), channel_id=1, source_target_pairs={{8,0},{16,8},{24,16},{9,1},{17,9},{25,17},{10,2},{18,10},{26,18},{... | collective-permute-start | bytes 73736 | tf_op jit(solution)/shard_map/ppermute | solution.py:21
  168.5 11.7 %collective-permute-start.5 = (bf16[24,512]{1,0:T(8,128)(2,1)S(1)}, bf16[24,512]{1,0:T(8,128)(2,1)S(1)}, u32[]{:S(2)}, u32[]{:S(2)}) collective-permute-start(bf16[24,512]{1,0:T(8,128)(2,1)S(1)} %get-tuple-element.63), channel_id=1, source_target_pairs={{7,0},{0,1},{1,2},{2,3},{3,4},{4,5},{5,6},{6,7},{15,8},{8,9},{9,10... | collective-permute-start | bytes 73736 | tf_op jit(solution)/shard_map/ppermute | solution.py:15
  168.6 23.9 %copy-start.1 = (bf16[512,512]{1,0:T(8,128)(2,1)S(1)}, bf16[512,512]{1,0:T(8,128)(2,1)}, u32[]{:S(2)}) copy-start(bf16[512,512]{1,0:T(8,128)(2,1)} %param.28) | copy-start | bytes 1572868
